TPU v7x, 32 devices: a whole 2x2x4 slice. The times are simulated.
32 devices in a mesh: band: 8 (over y, x, core), bus: 4 (over z).
Axes of the slice: x: 2, y: 2, z: 4, core: 2. Of those that a mesh axis runs over, the one named last changes fastest.
Arguments:
- dispatch0: float32 [64, 5120], P(None, ('band', 'bus')), may hold values from 0 to 1
- cost_lin: float32 [5120], P(('band', 'bus')), may hold values from -1 to 1
- cost_quad: float32 [5120], P(('band', 'bus')), may hold values from 0.5 to 4
- gen_max: float32 [5120], P(('band', 'bus')), may hold values from 0.5 to 2
- bus_map: int32 [5120], P(('band', 'bus')), may hold values from 0 to 98303, as said below
- demand: float32 [64, 4, 24576], P(None, 'bus', 'band'), may hold values from -6 to 6
- ptdf: float32 [2048, 98304], P('band', 'bus'), may hold values from -0.01953125 to 0.01953125
- line_price0: float32 [64, 2048], P(None, 'band'), may hold values from -3 to 3
- flow_max: float32 [2048], P('band'), may hold values from 0.3 to 3
Outputs:
- dispatch: float32 [64, 5120], P(None, ('band', 'bus'))
- line_price: float32 [64, 2048], P(None, 'band')
Inputs may be any that keep to these rules, and one draw needn't show every extreme that they name: `bus_map`: call bus 24576 * j + 3072 * i + k with 0 <= k < 3072 a bus of sub-block (i, j). Among the 160 generators of one aligned block (generators 160 * d to 160 * d + 159), at most 6 are sited in one sub-block, and one sub-block holds exactly 6 generators of every block.
All inputs are finite; a program needn't handle non-finite values.
Results may differ from a plain program's by a relative error of at most 0.0003.
Values sent between devices are 32-bit elements; how exact they have to be, the bound alone decides.
A program may use at most 128 MiB of HBM per device.

v0:
```python
import jax
import jax.numpy as jnp
from jax import lax
from jax.sharding import PartitionSpec as P

ITERS = 2


primal_step = 0.5
dual_step = 1.0


def owner_slots(bus_map, bus_width, sub_width, bus_count, slot_cap):
    block = bus_map // bus_width
    within = bus_map % bus_width
    owner = within // sub_width * bus_count + block
    local = within % sub_width
    same = owner[:, None] == owner[None, :]
    earlier = lax.broadcasted_iota(jnp.int32, same.shape, 0) > lax.broadcasted_iota(
        jnp.int32, same.shape, 1
    )
    rank = jnp.sum((same & earlier).astype(jnp.int32), axis=1)
    return (owner * slot_cap + rank, local)


def pack_rows(values, target, total):
    return jnp.zeros((total, values.shape[1]), values.dtype).at[target].set(values)


def on_device(
    dispatch0, cost_lin, cost_quad, gen_max, bus_map, demand, ptdf, line_price0, flow_max
):
    band_count = lax.axis_size("band")
    bus_count = lax.axis_size("bus")
    owner_count = band_count * bus_count
    gen_count = bus_map.shape[0]
    slot_cap = (gen_count + owner_count - 1) // owner_count + 1
    total = owner_count * slot_cap
    scenarios = dispatch0.shape[0]
    sub_width = demand.shape[2]
    bus_width = ptdf.shape[1]
    target, local = owner_slots(bus_map, bus_width, sub_width, bus_count, slot_cap)
    site_code = (local + 1).astype(jnp.float32)
    load = demand[:, 0, :]
    line_price = line_price0
    dispatch = dispatch0
    code_out = pack_rows(site_code[:, None], target, total).reshape(owner_count, slot_cap)
    column_ids = None
    for iteration in range(ITERS):
        sent = pack_rows(dispatch.T, target, total).reshape(owner_count, slot_cap * scenarios)
        arrived, codes = (
            lax.all_to_all(sent, ("band", "bus"), split_axis=0, concat_axis=0, tiled=True),
            lax.all_to_all(code_out, ("band", "bus"), split_axis=0, concat_axis=0, tiled=True),
        )
        slot_local = jnp.maximum(codes.reshape(total) - 1.0, 0.0).astype(jnp.int32)
        spread = (
            jnp.zeros((sub_width, scenarios), jnp.float32)
            .at[slot_local]
            .add(arrived.reshape(total, scenarios))
        )
        injection = spread.T - load
        flow = lax.psum(
            lax.dot_general(
                lax.all_gather(injection, "band", axis=1, tiled=True),
                ptdf,
                (((1,), (1,)), ((), ())),
                precision=lax.Precision.HIGHEST,
                preferred_element_type=jnp.float32,
            ),
            "bus",
        )
        bound = dual_step * flow_max
        trial = line_price + dual_step * flow
        price_next = trial - jnp.clip(trial, -bound, bound)
        line_price, reflected = (price_next, 2.0 * price_next - line_price)
        if iteration == 0:
            gathered = lax.all_gather(slot_local, "band", axis=0, tiled=True)
            position = lax.broadcasted_iota(jnp.int32, gathered.shape, 0)
            column_ids = position // total * sub_width + gathered
        rows_columns = jnp.take(ptdf, column_ids, axis=1)
        slot_price = lax.psum_scatter(
            lax.dot_general(
                rows_columns,
                reflected,
                (((0,), (1,)), ((), ())),
                precision=lax.Precision.HIGHEST,
                preferred_element_type=jnp.float32,
            ),
            "band",
            scatter_dimension=0,
            tiled=True,
        )
        answer = slot_price.reshape(owner_count, slot_cap * scenarios)
        back = lax.all_to_all(answer, ("band", "bus"), split_axis=0, concat_axis=0, tiled=True)
        unit_price = back.reshape(total, scenarios)[target].T
        dispatch = jnp.clip(
            (dispatch - primal_step * (cost_lin[None, :] + unit_price))
            / (1.0 + primal_step * cost_quad[None, :]),
            0.0,
            gen_max[None, :],
        )
    return (dispatch, line_price)


def solution(mesh):
    in_specs = (
        P(None, ("band", "bus")),
        P(("band", "bus")),
        P(("band", "bus")),
        P(("band", "bus")),
        P(("band", "bus")),
        P(None, "bus", "band"),
        P("band", "bus"),
        P(None, "band"),
        P("band"),
    )
    out_specs = (P(None, ("band", "bus")), P(None, "band"))
    return jax.shard_map(
        on_device, mesh=mesh, in_specs=in_specs, out_specs=out_specs, check_vma=False
    )
```

profile of v0, /device:TPU:0, one launch (start us, length us, event | category | flops | bytes accessed | tf_op | source)
XLA Modules:
  0.0 428.0 jit_solution(5949450486282528453)
XLA Ops:
  7.2 0.7 fusion.39
  7.9 0.2 convert_reduce_fusion
  8.1 1.1 scatter_custom_fusion
  9.2 0.7 all_to_all.31
  9.9 7.3 %all-to-all-start = ((f32[32,1,6]{2,1,0:T(1,128)}), f32[32,1,6]{2,1,0:T(1,128)S(1)}, u32[]{:S(2)}, u32[]{:S(2)}) async-start(f32[32,1,6]{2,1,0:T(1,128)} %bitcast), calls=%async_computation | async-start | bytes 32768 | tf_op jit(solution)/shard_map/all_to_all | solution.py:53
  17.3 2.3 copy.38
  19.7 1.0 scatter_custom_fusion.1
  20.7 0.7 all_to_all.41
  21.4 3.0 all-to-all-done
  24.4 2.9 all-to-all-start.1
  27.5 7.2 %all-to-all-done.1 = f32[32,1,384]{2,1,0:T(1,128)S(1)} async-done(((f32[32,1,384]{2,1,0:T(1,128)}), f32[32,1,384]{2,1,0:T(1,128)S(1)}, u32[]{:S(2)}, u32[]{:S(2)}) %all-to-all-start.1) | async-done | bytes 49184 | tf_op jit(solution)/shard_map/all_to_all | solution.py:52
  34.7 0.1 reduce.2
  34.9 1.6 scatter_custom_fusion.2
  36.5 1.3 bitcast_subtract_fusion.1
  37.9 25.0 %copy.35 = f32[256,24576]{0,1:T(8,128)} copy(f32[256,24576]{1,0:T(8,128)} %param.17) | data formatting | bytes 50331648 | tf_op args[6]
  62.9 0.6 dynamic-slice
  64.3 0.3 dynamic-update-slice
  64.6 6.6 %all-reduce = s32[1536]{0:T(1024)S(1)} all-reduce(s32[1536]{0:T(1024)S(1)} %dynamic-update-slice), channel_id=1, replica_groups=mesh['band'=8,'bus'=4] {'band'}, use_global_device_ids=true, to_apply=%add | all-reduce | flops 1536 | bytes 12288
  71.2 35.3 %all-gather.3.cloned.1.call-done = f32[64,24576]{0,1:T(8,128)} async-done(((f32[64,3072]{0,1:T(8,128)}), f32[64,24576]{0,1:T(8,128)}) %all-gather.3.cloned.1.call-update) | async-done | bytes 6291472 | tf_op jit(solution)/shard_map/all_gather | solution.py:64
  106.5 27.7 %fusion.48 = f32[64,256]{1,0:T(8,128)} fusion(f32[64,24576]{0,1:T(8,128)} %all-gather.3.cloned.1.call-done, f32[256,24576]{1,0:T(8,128)} %param.17), kind=kOutput, calls=%fused_computation.81 | convolution fusion | flops 4831838208 | bytes 31522816 | tf_op jit(solution)/shard_map/dot_general | solution.py:63
  134.2 0.3 reduce-scatter.7.cloned.1.call-start
  134.5 11.9 %gather_fusion.2 = f32[1536,256]{1,0:T(8,128)S(1)} fusion(f32[256,24576]{0,1:T(8,128)} %copy.35, s32[2048]{0:T(1024)S(1)} %pad_clamp_fusion), kind=kCustom, calls=%fused_computation.clone | custom fusion | bytes 3151872 | tf_op jit(solution)/shard_map/jit(_take)/gather | solution.py:80
  146.4 22.2 %all-reduce.4.cloned.1.call-done = f32[64,256]{1,0:T(8,128)} async-done(((f32[64,256]{1,0:T(8,128)}), f32[64,256]{1,0:T(8,128)}) %all-reduce.4.cloned.1.call-update) | async-done | bytes 65552 | tf_op jit(solution)/shard_map/psum | solution.py:62
  168.6 3.2 fusion.2
  171.9 34.7 %reduce-scatter.7.cloned.1.call-done = f32[192,64]{1,0:T(8,128)} async-done(((f32[1536,64]{1,0:T(8,128)}), f32[192,64]{1,0:T(8,128)}) %reduce-scatter.7.cloned.1.call-update) | async-done | bytes 49168 | tf_op jit(solution)/shard_map/reduce_scatter | solution.py:81
  206.6 1.6 all_to_all.42
  208.2 4.6 %all-to-all-start.2 = ((f32[32,1,384]{2,1,0:T(1,128)}), f32[32,1,384]{2,1,0:T(1,128)S(1)}, u32[]{:S(2)}, u32[]{:S(2)}) async-start(f32[32,1,384]{2,1,0:T(1,128)} %all_to_all.42), calls=%async_computation.2 | async-start | bytes 98304 | tf_op jit(solution)/shard_map/all_to_all | solution.py:94
  212.9 7.3 %all-to-all-done.2 = f32[32,1,384]{2,1,0:T(1,128)S(1)} async-done(((f32[32,1,384]{2,1,0:T(1,128)}), f32[32,1,384]{2,1,0:T(1,128)S(1)}, u32[]{:S(2)}, u32[]{:S(2)}) %all-to-all-start.2) | async-done | bytes 49184 | tf_op jit(solution)/shard_map/all_to_all | solution.py:94
  220.2 0.1 reduce.3
  220.4 0.7 gather_fusion
  221.1 1.1 scatter_custom_fusion.3
  222.3 9.1 %all_to_all.50 = f32[32,1,384]{2,1,0:T(1,128)S(1)} all-to-all(f32[32,1,384]{2,1,0:T(1,128)S(1)} %all_to_all.43), channel_id=1, replica_groups=mesh['band'=8,'bus'=4] {'band','bus'}, dimensions={0} | all-to-all | bytes 98304 | tf_op jit(solution)/shard_map/all_to_all | solution.py:52
  231.4 0.1 reduce.4
  231.5 0.7 reshape.159
  232.2 2.8 scatter_custom_fusion.4
  235.1 2.8 bitcast_subtract_fusion
  237.9 68.5 %all-gather.5.cloned.1.call-done = f32[64,24576]{0,1:T(8,128)} async-done(((f32[64,3072]{0,1:T(8,128)}), f32[64,24576]{0,1:T(8,128)}) %all-gather.5.cloned.1.call-update) | async-done | bytes 6291472 | tf_op jit(solution)/shard_map/all_gather | solution.py:64
  306.4 27.7 %fusion.49 = f32[64,256]{1,0:T(8,128)} fusion(f32[64,24576]{0,1:T(8,128)} %all-gather.5.cloned.1.call-done, f32[256,24576]{1,0:T(8,128)} %param.17), kind=kOutput, calls=%fused_computation.82 | convolution fusion | flops 4831838208 | bytes 31522816 | tf_op jit(solution)/shard_map/dot_general | solution.py:63
  334.2 34.4 %all-reduce.6.cloned.1.call-done = f32[64,256]{1,0:T(8,128)} async-done(((f32[64,256]{1,0:T(8,128)}), f32[64,256]{1,0:T(8,128)}) %all-reduce.6.cloned.1.call-update) | async-done | bytes 65552 | tf_op jit(solution)/shard_map/psum | solution.py:62
  368.6 0.9 minimum_subtract_fusion
  369.5 2.3 fusion
  371.8 34.8 %reduce-scatter.9.cloned.1.call-done = f32[192,64]{1,0:T(8,128)} async-done(((f32[1536,64]{1,0:T(8,128)}), f32[192,64]{1,0:T(8,128)}) %reduce-scatter.9.cloned.1.call-update) | async-done | bytes 49168 | tf_op jit(solution)/shard_map/reduce_scatter | solution.py:81
  406.6 1.0 all_to_all.44
  407.6 11.8 %all_to_all.51 = f32[32,1,384]{2,1,0:T(1,128)S(1)} all-to-all(f32[32,1,384]{2,1,0:T(1,128)S(1)} %all_to_all.44), channel_id=1, replica_groups=mesh['band'=8,'bus'=4] {'band','bus'}, dimensions={0} | all-to-all | bytes 98304 | tf_op jit(solution)/shard_map/all_to_all | solution.py:94
  419.4 0.1 reduce.5
  419.6 0.7 gather_fusion.1
  420.3 0.1 fusion.17
  420.4 0.7 copy.45
  (49 shorter events, 1.2 us)
Async XLA Ops:
  7.2 12.4 %copy-start.2 = (f32[64,160]{1,0:T(8,128)S(1)}, f32[64,160]{1,0:T(8,128)}, u32[]{:S(2)}) copy-start(f32[64,160]{1,0:T(8,128)} %param.11) | copy-start | bytes 122884
  9.9 14.5 %all-to-all-start = ((f32[32,1,6]{2,1,0:T(1,128)}), f32[32,1,6]{2,1,0:T(1,128)S(1)}, u32[]{:S(2)}, u32[]{:S(2)}) async-start(f32[32,1,6]{2,1,0:T(1,128)} %bitcast), calls=%async_computation | async-start | bytes 32768 | tf_op jit(solution)/shard_map/all_to_all | solution.py:53
  24.4 10.3 %all-to-all-start.1 = ((f32[32,1,384]{2,1,0:T(1,128)}), f32[32,1,384]{2,1,0:T(1,128)S(1)}, u32[]{:S(2)}, u32[]{:S(2)}) async-start(f32[32,1,384]{2,1,0:T(1,128)} %all_to_all.41), calls=%async_computation.1 | async-start | bytes 98304 | tf_op jit(solution)/shard_map/all_to_all | solution.py:52
  27.3 79.2 %all-gather.3.cloned.1.call-start = ((), (), s32[]{:S(2)}) async-start(), calls=%async_computation.7 | async-start | bytes 14155776 | tf_op jit(solution)/shard_map/all_gather | solution.py:64
  27.5 10.3 %copy-start.8 = (s32[192,1]{0,1:T(1,128)}, s32[192,1]{0,1:T(1,128)S(1)}, u32[]{:S(2)}) copy-start(s32[192,1]{0,1:T(1,128)S(1)} %compare_select_fusion.1) | copy-start | bytes 2308
  37.8 130.8 %all-reduce.4.cloned.1.call-start = ((), (), s32[]{:S(2)}) async-start(), calls=%async_computation.8 | async-start | bytes 131072 | tf_op jit(solution)/shard_map/psum | solution.py:62
  37.9 25.0 %copy-start.4 = (f32[256]{0:T(256)S(1)}, f32[256]{0:T(256)}, u32[]{:S(2)}) copy-start(f32[256]{0:T(256)} %param.19) | copy-start | bytes 3076
  37.9 25.0 %copy-start.9 = (u32[32]{0:T(128)S(1)}, u32[32]{0:T(128)}, u32[]{:S(2)}) copy-start(u32[32]{0:T(128)} %constant.80) | copy-start | bytes 388
  134.2 72.3 %reduce-scatter.7.cloned.1.call-start = ((), (), s32[]{:S(2)}) async-start(), calls=%async_computation.11 | async-start | bytes 884736 | tf_op jit(solution)/shard_map/reduce_scatter | solution.py:81
  134.5 34.1 %copy-start = (f32[64,256]{1,0:T(8,128)S(1)}, f32[64,256]{1,0:T(8,128)}, u32[]{:S(2)}) copy-start(f32[64,256]{1,0:T(8,128)} %param.18) | copy-start | bytes 196612
  168.6 3.3 copy-start.7
  171.8 49.3 %copy-start.5 = (f32[160]{0:T(256)S(1)}, f32[160]{0:T(256)}, u32[]{:S(2)}) copy-start(f32[160]{0:T(256)} %param.12) | copy-start | bytes 1924
  171.8 49.3 %copy-start.6 = (f32[160]{0:T(256)S(1)}, f32[160]{0:T(256)}, u32[]{:S(2)}) copy-start(f32[160]{0:T(256)} %param.14) | copy-start | bytes 1924
  208.2 12.0 %all-to-all-start.2 = ((f32[32,1,384]{2,1,0:T(1,128)}), f32[32,1,384]{2,1,0:T(1,128)S(1)}, u32[]{:S(2)}, u32[]{:S(2)}) async-start(f32[32,1,384]{2,1,0:T(1,128)} %all_to_all.42), calls=%async_computation.2 | async-start | bytes 98304 | tf_op jit(solution)/shard_map/all_to_all | solution.py:94
  212.8 93.6 %all-gather.5.cloned.1.call-start = ((), (), s32[]{:S(2)}) async-start(), calls=%async_computation.9 | async-start | bytes 14155776 | tf_op jit(solution)/shard_map/all_gather | solution.py:64
  237.9 130.7 %copy-start.1 = (f32[64,256]{1,0:T(8,128)S(1)}, f32[64,256]{1,0:T(8,128)}, u32[]{:S(2)}) copy-start(f32[64,256]{1,0:T(8,128)} %all-reduce.4.cloned.1.call-done) | copy-start | bytes 196612
  237.9 130.7 %all-reduce.6.cloned.1.call-start = ((), (), s32[]{:S(2)}) async-start(), calls=%async_computation.10 | async-start | bytes 131072 | tf_op jit(solution)/shard_map/psum | solution.py:62
  334.1 72.5 %reduce-scatter.9.cloned.1.call-start = ((), (), s32[]{:S(2)}) async-start(), calls=%async_computation.12 | async-start | bytes 884736 | tf_op jit(solution)/shard_map/reduce_scatter | solution.py:81
  369.5 2.4 copy-start.3
Sparse Core Ops, SparseCore 0:
  37.9 68.5 all-gather.2
  134.3 34.2 all-reduce.3
  171.9 34.6 reduce-scatter.6
  238.0 68.3 all-gather.4
  334.3 34.2 all-reduce.5
  371.9 34.6 reduce-scatter.8
where the time goes:
time: 429 us; the launch traced here: 428 us
  waiting for transfers between devices  247 us (58%)
  matrix products  60.9 us (14%)
  local copies, waits for them, and re-layouts  49.7 us (12%)
  blocking collectives  27.5 us (6%)
  starting transfers between devices  15.3 us (4%)
  between operations  15.1 us (4%)
  other arithmetic  12.1 us (3%)
    all_gather x2, waiting for transfers between devices, on_device(): lax.all_gather(injection, 'band', axis=1, tiled=True)  104 us
    reduce_scatter x2, waiting for transfers between devices, on_device(): lax.psum_scatter(lax.dot_general(rows_columns, reflected, (((0,), (1,)),...  69.4 us
    psum x2, waiting for transfers between devices, on_device(): lax.psum(lax.dot_general(lax.all_gather(injection, 'band', axis=1, tiled=...  56.6 us
    dot_general x2, matrix products, on_device(): lax.dot_general(lax.all_gather(injection, 'band', axis=1, tiled=True), pt...  55.4 us
    unnamed x26, local copies, waits for them, and re-layouts  29 us
    gather x1, local copies, waits for them, and re-layouts, on_device(): rows_columns = jnp.take(ptdf, column_ids, axis=1)  11.9 us
    all_to_all x1, blocking collectives, on_device(): lax.all_to_all(answer, ('band', 'bus'), split_axis=0, concat_axis=0, tile...  11.8 us
    all_to_all x1, blocking collectives, on_device(): lax.all_to_all(sent, ('band', 'bus'), split_axis=0, concat_axis=0, tiled=...  9.09 us
  transfers between devices with their start and end apart: 9, of which 9 were waited for; matrix products, arithmetic and copies ran while one was open for 10% of the time, Pallas kernels for 0%

commit v1 on v0

v1 whole, which is shorter than its diff:
```python
import functools
import jax
import jax.numpy as jnp
from jax import lax
from jax.experimental import pallas as pl
from jax.experimental.pallas import tpu as pltpu
from jax.sharding import PartitionSpec as P

ITERS = 2
ROWS = 8
LANES = 128
MESH = pl.DeviceIdType.MESH

primal_step = 0.5
dual_step = 1.0

NT = (((1,), (1,)), ((), ()))
NN = (((1,), (0,)), ((), ()))


def owner_slots(bus_map, bus_width, sub_width, bus_count):
    block = bus_map // bus_width
    within = bus_map % bus_width
    owner = within // sub_width * bus_count + block
    local = within % sub_width
    same = owner[:, None] == owner[None, :]
    earlier = lax.broadcasted_iota(jnp.int32, same.shape, 0) > lax.broadcasted_iota(
        jnp.int32, same.shape, 1
    )
    rank = jnp.sum((same & earlier).astype(jnp.int32), axis=1)
    return (owner * ROWS + rank, local)


def split(x):
    hi = x.astype(jnp.bfloat16)
    lo = (x - hi.astype(jnp.float32)).astype(jnp.bfloat16)
    return hi, lo


def dot(a, b, dims):
    return lax.dot_general(a, b, dims, preferred_element_type=jnp.float32)


def flip(i, m, bits):
    r = i
    for b in range(bits):
        w = 1 << b
        ib = (i // w) % 2
        mb = (m // w) % 2
        r = r + w * mb * (1 - 2 * ib)
    return r


def market_kernel(
    nb, nz, cap, depth, kt,
    pack_ref, dem_ref, ptdf_ref, lp0_ref, fmax_ref,
    ret_ref, lp_ref,
    pin, slots, dem, pbuf, acc1, acc2, ghi, glo, lf, zbuf, dbuf, pps, ppr, rout, rin,
    dloc_sem, p_sem, a_send, a_recv, dem_send, dem_recv, fw_send,
    z_send, z_recv, d_send, d_recv, pp_send, pp_recv, r_send, r_recv,
):
    i = lax.axis_index("band")
    j = lax.axis_index("bus")
    n = nb * nz
    me = i * nz + j
    bits = nb.bit_length() - 1
    scen = lp0_ref.shape[0]
    lines = lp0_ref.shape[1]
    sub = dem_ref.shape[1]
    s_count = n * cap
    partner = i + 1 - 2 * (i % 2)

    def pcopy(m):
        o = flip(i, m, bits)
        return pltpu.make_async_copy(
            ptdf_ref.at[:, pl.ds(pl.multiple_of(o * sub, LANES), sub)],
            pbuf.at[m % depth],
            p_sem.at[m % depth],
        )

    @pl.loop(0, depth)
    def _(m):
        pcopy(m).start()

    dloc = pltpu.make_async_copy(dem_ref, dem.at[i], dloc_sem.at[0])
    dloc.start()
    ploc = pltpu.make_async_copy(pack_ref.at[me], pin.at[me], dloc_sem.at[1])
    ploc.start()

    barrier = pltpu.get_barrier_semaphore()

    @pl.loop(1, n)
    def _(k):
        d = (me + k) % n
        pl.semaphore_signal(barrier, inc=1, device_id=(d // nz, d % nz), device_id_type=MESH)

    pl.semaphore_wait(barrier, n - 1)

    def acopy(d, s):
        return pltpu.make_async_remote_copy(
            src_ref=pack_ref.at[d], dst_ref=pin.at[s], send_sem=a_send.at[d], recv_sem=a_recv.at[s],
            device_id=(d // nz, d % nz), device_id_type=MESH,
        )

    @pl.loop(1, n)
    def _(k):
        acopy((me + k) % n, me).start()

    def dcopy(m):
        to = flip(i, m, bits)
        return pltpu.make_async_remote_copy(
            src_ref=dem_ref, dst_ref=dem.at[i], send_sem=dem_send.at[m], recv_sem=dem_recv.at[i],
            device_id=(to, j), device_id_type=MESH,
        )

    def fcopy(m):
        o = flip(i, m, bits)
        return pltpu.make_async_remote_copy(
            src_ref=dem.at[o], dst_ref=dem.at[o], send_sem=fw_send.at[m], recv_sem=dem_recv.at[o],
            device_id=(partner, j), device_id_type=MESH,
        )

    dcopy(1).start()
    for m in range(2, nb, 2):
        dcopy(m).start()

    @pl.loop(1, n)
    def _(k):
        s = (me + k) % n
        acopy(s, s).wait_recv()

    ploc.wait()
    if cap == ROWS:
        slots[...] = pin[...].reshape(s_count, LANES)
    else:
        for d in range(n):
            slots[d * cap:(d + 1) * cap, :] = pin[d, 0:cap, :]
    pack_t = slots[...].T
    lin = pack_t[scen:scen + 1, :]
    quad = pack_t[scen + 1:scen + 2, :]
    gmax = pack_t[scen + 2:scen + 3, :]
    dbuf[0, i] = pack_t[0:scen, :]

    def gcopy(it, m):
        to = flip(i, m, bits)
        return pltpu.make_async_remote_copy(
            src_ref=dbuf.at[it, i], dst_ref=dbuf.at[it, i],
            send_sem=d_send.at[it, m], recv_sem=d_recv.at[it, i],
            device_id=(to, j), device_id_type=MESH,
        )

    def gwait(it, m):
        o = flip(i, m, bits)
        return pltpu.make_async_remote_copy(
            src_ref=dbuf.at[it, o], dst_ref=dbuf.at[it, o],
            send_sem=d_send.at[it, m], recv_sem=d_recv.at[it, o],
            device_id=(o, j), device_id_type=MESH,
        )

    @pl.loop(1, nb)
    def _(m):
        gcopy(0, m).start()

    dloc.wait()
    lf[...] = jnp.zeros_like(lf)
    lane = lax.broadcasted_iota(jnp.int32, (s_count, LANES), 1)
    at_lane = lax.broadcasted_iota(jnp.int32, (s_count, kt), 1).astype(jnp.float32) + 1.0

    @pl.loop(0, nb)
    def _(m):
        o = flip(i, m, bits)

        @pl.when(m > 0)
        def _():
            fcopy(m).wait_recv()

        @pl.when((m > 0) & (m % 2 == 0))
        def _():
            fcopy(m).start()

        pcopy(m).wait()
        codes = jnp.sum(jnp.where(lane == LANES - nb + o, slots[...], 0.0), axis=1, keepdims=True)
        for t in range(sub // kt):
            cols = slice(t * kt, (t + 1) * kt)
            ph, plo = split(pbuf[m % depth, :, cols])
            dh, dl = split(dem[o, :, cols])
            oh = jnp.where(at_lane == codes - float(t * kt), 1.0, 0.0).astype(jnp.bfloat16)
            one = dot(jnp.concatenate([dh, dl, oh], axis=0), ph, NT)
            two = dot(jnp.concatenate([dh, oh], axis=0), plo, NT)
            if t == 0:
                acc1[...] = one
                acc2[...] = two
            else:
                acc1[...] += one
                acc2[...] += two
        lf[...] += (acc1[scen:2 * scen, :] + acc2[0:scen, :]) + acc1[0:scen, :]
        ghi[o] = acc1[2 * scen:2 * scen + s_count, :].astype(jnp.bfloat16)
        glo[o] = acc2[scen:scen + s_count, :].astype(jnp.bfloat16)

        @pl.when(m + depth < nb)
        def _():
            pcopy(m + depth).start()

    price = lp0_ref[...]
    bound = dual_step * fmax_ref[...]

    for it in range(ITERS):
        zbuf[it, j] = -lf[...]

        def add_flow(m, it=it):
            o = flip(i, m, bits)
            dh, dl = split(dbuf[it, o])
            both = dot(jnp.concatenate([dh, dl], axis=0), ghi[o], NN)
            zbuf[it, j] += both[scen:, :] + dot(dh, glo[o], NN) + both[0:scen, :]

        add_flow(0)

        @pl.loop(1, nb)
        def _(m, it=it):
            gwait(it, m).wait_recv()
            add_flow(m)

        def zcopy(k, it=it):
            to = (j + k) % nz
            return pltpu.make_async_remote_copy(
                src_ref=zbuf.at[it, j], dst_ref=zbuf.at[it, j],
                send_sem=z_send.at[it, k], recv_sem=z_recv.at[it, j],
                device_id=(i, to), device_id_type=MESH,
            )

        def zwait(k, it=it):
            o = (j + k) % nz
            return pltpu.make_async_remote_copy(
                src_ref=zbuf.at[it, o], dst_ref=zbuf.at[it, o],
                send_sem=z_send.at[it, k], recv_sem=z_recv.at[it, o],
                device_id=(i, o), device_id_type=MESH,
            )

        for k in range(1, nz):
            zcopy(k).start()
        for k in range(1, nz):
            zwait(k).wait_recv()
        flow = zbuf[it, 0]
        for k in range(1, nz):
            flow = flow + zbuf[it, k]
        trial = price + dual_step * flow
        price_next = trial - jnp.clip(trial, -bound, bound)
        reflected = 2.0 * price_next - price
        price = price_next

        rh, rl = split(reflected)
        rhl = jnp.concatenate([rh, rl], axis=0)

        def slot_price(o):
            both = dot(rhl, ghi[o], NT)
            return both[scen:, :] + dot(rh, glo[o], NT) + both[0:scen, :]

        def ppcopy(m, it=it):
            o = flip(i, m, bits)
            return pltpu.make_async_remote_copy(
                src_ref=pps.at[o], dst_ref=ppr.at[it, i],
                send_sem=pp_send.at[it, m], recv_sem=pp_recv.at[it, i],
                device_id=(o, j), device_id_type=MESH,
            )

        def ppwait(m, it=it):
            o = flip(i, m, bits)
            return pltpu.make_async_remote_copy(
                src_ref=pps.at[o], dst_ref=ppr.at[it, o],
                send_sem=pp_send.at[it, m], recv_sem=pp_recv.at[it, o],
                device_id=(o, j), device_id_type=MESH,
            )

        @pl.loop(0, nb - 1)
        def _(k):
            m = nb - 1 - k
            o = flip(i, m, bits)
            pps[o] = slot_price(o)
            ppcopy(m).start()

        ppr[it, i] = slot_price(i)

        @pl.loop(1, nb)
        def _(m):
            ppwait(m).wait_recv()
            ppcopy(m).wait_send()

        unit = ppr[it, 0]
        for s in range(1, nb):
            unit = unit + ppr[it, s]
        held = dbuf[it, i]
        held = jnp.clip(
            (held - primal_step * (lin + unit)) / (1.0 + primal_step * quad), 0.0, gmax
        )
        if it < ITERS - 1:
            dbuf[it + 1, i] = held

            @pl.loop(1, nb)
            def _(m, it=it):
                gcopy(it + 1, m).start()

    lp_ref[...] = price
    back = jnp.concatenate([held, jnp.zeros((LANES - scen, s_count), jnp.float32)], axis=0).T
    if cap == ROWS:
        rout[...] = back.reshape(n, ROWS, LANES)
    else:
        rout[...] = jnp.zeros_like(rout)
        slots[...] = back
        for d in range(n):
            rout[d, 0:cap, :] = slots[d * cap:(d + 1) * cap, :]

    def rcopy(d, s):
        return pltpu.make_async_remote_copy(
            src_ref=rout.at[d], dst_ref=rin.at[s], send_sem=r_send.at[d], recv_sem=r_recv.at[s],
            device_id=(d // nz, d % nz), device_id_type=MESH,
        )

    @pl.loop(1, n)
    def _(k):
        rcopy((me + k) % n, me).start()

    dcopy(1).wait_send()
    for m in range(2, nb, 2):
        dcopy(m).wait_send()
        fcopy(m).wait_send()

    @pl.loop(1, nb)
    def _(m):
        for it in range(ITERS):
            gcopy(it, m).wait_send()

    for it in range(ITERS):
        for k in range(1, nz):
            pltpu.make_async_remote_copy(
                src_ref=zbuf.at[it, j], dst_ref=zbuf.at[it, j],
                send_sem=z_send.at[it, k], recv_sem=z_recv.at[it, j],
                device_id=(i, (j + k) % nz), device_id_type=MESH,
            ).wait_send()

    ret_ref[me] = rout[me]

    @pl.loop(1, n)
    def _(k):
        d = (me + k) % n
        acopy(d, d).wait_send()
        rcopy(d, d).wait_recv()
        rcopy(d, d).wait_send()
        ret_ref[d] = rin[d]


def on_device(
    dispatch0, cost_lin, cost_quad, gen_max, bus_map, demand, ptdf, line_price0, flow_max
):
    nb = lax.axis_size("band")
    nz = lax.axis_size("bus")
    n = nb * nz
    gens = bus_map.shape[0]
    scen = dispatch0.shape[0]
    sub = demand.shape[2]
    lines = ptdf.shape[0]
    cap = (gens + n - 1) // n + 1
    while n * cap % LANES:
        cap += 1
    s_count = n * cap
    assert cap <= ROWS and scen + 4 + nb <= LANES and nb & (nb - 1) == 0
    target, local = owner_slots(bus_map, ptdf.shape[1], sub, nz)
    body = jnp.concatenate(
        [
            dispatch0,
            cost_lin[None, :],
            cost_quad[None, :],
            gen_max[None, :],
            (local + 1).astype(jnp.float32)[None, :],
        ],
        axis=0,
    ).T
    rows = jnp.zeros((n * ROWS, scen + 4), jnp.float32).at[target].set(body).reshape(n, ROWS, scen + 4)
    codes = rows[:, :, scen + 3].reshape(nb, nz, ROWS).transpose(1, 2, 0)
    codes = jnp.broadcast_to(codes[None], (nb, nz, ROWS, nb)).reshape(n, ROWS, nb)
    pad = jnp.zeros((n, ROWS, LANES - nb - scen - 4), jnp.float32)
    pack = jnp.concatenate([rows, pad, codes], axis=2)

    depth = min(nb, 8)
    kt = sub
    while kt > 1024:
        kt //= 2
    if sub % kt or kt % LANES:
        kt = sub
    if sub % 1024 == 0:
        kt = 1024
    f32, bf16 = jnp.float32, jnp.bfloat16
    vmem = pl.BlockSpec(memory_space=pltpu.VMEM)
    dma = pltpu.SemaphoreType.DMA
    ret, line_price = pl.pallas_call(
        functools.partial(market_kernel, nb, nz, cap, depth, kt),
        out_shape=(
            jax.ShapeDtypeStruct((n, ROWS, LANES), f32),
            jax.ShapeDtypeStruct((scen, lines), f32),
        ),
        in_specs=[vmem, vmem, pl.BlockSpec(memory_space=pl.ANY), vmem, vmem],
        out_specs=(vmem, vmem),
        scratch_shapes=[
            pltpu.VMEM((n, ROWS, LANES), f32),
            pltpu.VMEM((s_count, LANES), f32),
            pltpu.VMEM((nb, scen, sub), f32),
            pltpu.VMEM((depth, lines, sub), f32),
            pltpu.VMEM((2 * scen + s_count, lines), f32),
            pltpu.VMEM((scen + s_count, lines), f32),
            pltpu.VMEM((nb, s_count, lines), bf16),
            pltpu.VMEM((nb, s_count, lines), bf16),
            pltpu.VMEM((scen, lines), f32),
            pltpu.VMEM((ITERS, nz, scen, lines), f32),
            pltpu.VMEM((ITERS, nb, scen, s_count), f32),
            pltpu.VMEM((nb, scen, s_count), f32),
            pltpu.VMEM((ITERS, nb, scen, s_count), f32),
            pltpu.VMEM((n, ROWS, LANES), f32),
            pltpu.VMEM((n, ROWS, LANES), f32),
            dma((2,)), dma((depth,)),
            dma((n,)), dma((n,)),
            dma((nb,)), dma((nb,)), dma((nb,)),
            dma((ITERS, nz)), dma((ITERS, nz)),
            dma((ITERS, nb)), dma((ITERS, nb)),
            dma((ITERS, nb)), dma((ITERS, nb)),
            dma((n,)), dma((n,)),
        ],
        compiler_params=pltpu.CompilerParams(
            collective_id=0, has_side_effects=True, vmem_limit_bytes=60 * 1024 * 1024
        ),
        name="market",
    )(pack, demand[:, 0, :], ptdf, line_price0, flow_max[None, :])
    dispatch = ret.reshape(n * ROWS, LANES)[target][:, :scen].T
    return (dispatch, line_price)


def solution(mesh):
    in_specs = (
        P(None, ("band", "bus")),
        P(("band", "bus")),
        P(("band", "bus")),
        P(("band", "bus")),
        P(("band", "bus")),
        P(None, "bus", "band"),
        P("band", "bus"),
        P(None, "band"),
        P("band"),
    )
    out_specs = (P(None, ("band", "bus")), P(None, "band"))
    return jax.shard_map(
        on_device, mesh=mesh, in_specs=in_specs, out_specs=out_specs, check_vma=False
    )
```

time: 429 us -> 110 us (0.26)
  waiting for transfers between devices: 247 us -> 0 us
  Pallas kernels: 0 us -> 98.5 us
  matrix products: 60.9 us -> 0 us
  local copies, waits for them, and re-layouts: 49.7 us -> 8.92 us
  blocking collectives: 27.5 us -> 0 us
  starting transfers between devices: 15.3 us -> 0 us
  between operations: 15.1 us -> 0.69 us
  other arithmetic: 12.1 us -> 1.66 us
    all_gather x2 -> x0, waiting for transfers between devices: 104 us -> none  [on_device(): lax.all_gather(injection, 'band', axis=1, tiled=True)]
    pallas_call x0 -> x1, Pallas kernels: none -> 98.5 us  [on_device(): pl.pallas_call(functools.partial(market_kernel, nb, nz, cap, depth, kt),...]
    reduce_scatter x2 -> x0, waiting for transfers between devices: 69.4 us -> none  [on_device(): lax.psum_scatter(lax.dot_general(rows_columns, reflected, (((0,), (1,)),...]
    psum x2 -> x0, waiting for transfers between devices: 56.6 us -> none  [on_device(): lax.psum(lax.dot_general(lax.all_gather(injection, 'band', axis=1, tiled=...]
    dot_general x2 -> x0, matrix products: 55.4 us -> none  [on_device(): lax.dot_general(lax.all_gather(injection, 'band', axis=1, tiled=True), pt...]
    unnamed x26 -> x3, local copies, waits for them, and re-layouts: 29 us -> 4.34 us
    all_to_all x2 -> x0, blocking collectives: 20.9 us -> none  [the longest x1 11.8 us: on_device(): lax.all_to_all(answer, ('band', 'bus'), split_axis=0, concat_axis=0, tile...]
    all_to_all x3 -> x0, waiting for transfers between devices: 17.5 us -> none  [the longest x1 7.33 us: on_device(): lax.all_to_all(answer, ('band', 'bus'), split_axis=0, concat_axis=0, tile...]
  transfers between devices with their start and end apart: 9 -> 0, of which waited for: 9 -> 0; matrix products, arithmetic and copies ran while one was open for 10% -> 0% of each run, Pallas kernels for 0% -> 0%
where the time goes in v1:
time: 110 us
  Pallas kernels  98.5 us (90%)
  local copies, waits for them, and re-layouts  8.92 us (8%)
  other arithmetic  1.66 us (2%)
    pallas_call x1, Pallas kernels, on_device(): pl.pallas_call(functools.partial(market_kernel, nb, nz, cap, depth, kt),...  98.5 us
    unnamed x3, local copies, waits for them, and re-layouts  4.34 us

profile of v1, /device:TPU:0, one launch (start us, length us, event | category | flops | bytes accessed | tf_op | source)
XLA Modules:
  0.0 109.8 jit_solution(4008859434095462675)
XLA Ops:
  0.6 0.7 fusion.5
  1.3 0.2 convert_reduce_fusion
  1.5 1.6 %concatenate.6 = f32[68,160]{1,0:T(8,128)S(1)} concatenate(f32[64,160]{1,0:T(8,128)} %param.9, f32[1,160]{1,0:T(1,128)} %bitcast.25, f32[1,160]{1,0:T(1,128)} %bitcast.26, f32[1,160]{1,0:T(1,128)} %bitcast.27, f32[1,160]{1,0:T(1,128)S(1)} %bitcast.24), dimensions={0} | concatenate | bytes 87040 | tf_op jit(solution)/shard_map/concatenate | solution.py:367
  3.1 0.1 copy.17
  3.2 1.0 scatter_custom_fusion
  4.2 0.2 slice_reduce_fusion
  4.4 0.1 copy.18
  4.5 0.1 pad.1.clone
  4.6 0.8 pad_maximum_fusion.pack_ref
  5.3 2.1 %copy.22 = f32[64,1,3072]{2,0,1:T(8,128)} copy(f32[64,1,3072]{2,1,0:T(1,128)} %param.14) | data formatting | bytes 1572864
  7.5 98.5 %market.1 = (f32[32,8,128]{2,1,0:T(8,128)}, f32[64,256]{1,0:T(8,128)}) custom-call(f32[32,8,128]{2,1,0:T(8,128)} %pad_maximum_fusion.pack_ref, f32[64,3072]{1,0:T(8,128)} %bitcast.18, f32[256,24576]{1,0:T(8,128)} %ptdf_ref.1, f32[64,256]{1,0:T(8,128)} %lp0_ref.1, f32[1,256]{1,0:T(1,128)} %bitcast.28), custom_call_target="tpu_custom_call" | custom-call | tf_op jit(solution)/shard_map/market/pallas_call | solution.py:394
  106.0 1.6 %gather_fusion = f32[160,128]{1,0:T(8,128)S(1)} fusion(f32[256,128]{1,0:T(8,128)} %bitcast.17, s32[1024]{0:T(1024)S(1)} %pad_clamp_fusion), kind=kCustom, calls=%fused_computation | custom fusion | bytes 164480 | tf_op jit(solution)/shard_map/gather | solution.py:431
  107.6 0.7 copy.19
  108.3 1.5 %copy.24 = f32[64,256]{1,0:T(8,128)} copy(f32[64,256]{1,0:T(8,128)} %get-tuple-element.17) | data formatting | bytes 131072
  (5 shorter events, 0.0 us)

commit v2 on v1

--- a/solution.py
+++ b/solution.py
@@ -16,19 +16,6 @@
 
 NT = (((1,), (1,)), ((), ()))
 NN = (((1,), (0,)), ((), ()))
-
-
-def owner_slots(bus_map, bus_width, sub_width, bus_count):
-    block = bus_map // bus_width
-    within = bus_map % bus_width
-    owner = within // sub_width * bus_count + block
-    local = within % sub_width
-    same = owner[:, None] == owner[None, :]
-    earlier = lax.broadcasted_iota(jnp.int32, same.shape, 0) > lax.broadcasted_iota(
-        jnp.int32, same.shape, 1
-    )
-    rank = jnp.sum((same & earlier).astype(jnp.int32), axis=1)
-    return (owner * ROWS + rank, local)
 
 
 def split(x):
@@ -53,11 +40,11 @@
 
 def market_kernel(
     nb, nz, cap, depth, kt,
-    pack_ref, dem_ref, ptdf_ref, lp0_ref, fmax_ref,
-    ret_ref, lp_ref,
-    pin, slots, dem, pbuf, acc1, acc2, ghi, glo, lf, zbuf, dbuf, pps, ppr, rout, rin,
-    dloc_sem, p_sem, a_send, a_recv, dem_send, dem_recv, fw_send,
-    z_send, z_recv, d_send, d_recv, pp_send, pp_recv, r_send, r_recv,
+    disp_ref, par_ref, bus_ref, dem_ref, ptdf_ref, lp0_ref, fmax_ref,
+    out_ref, lp_ref,
+    pack, pin, slots, dem, pbuf, acc1, acc2, ghi, glo, lf, zbuf, dbuf, pps, ppx, ppr, rout, rin,
+    dloc_sem, p_sem, a_send, a_recv, dem_send, dem_recv, fw_send, fw_recv, rel_send,
+    z_send, z_recv, d_send, d_recv, df_send, px_send, px_recv, pp_send, pp_recv, r_send, r_recv,
 ):
     i = lax.axis_index("band")
     j = lax.axis_index("bus")
@@ -66,7 +53,10 @@
     bits = nb.bit_length() - 1
     scen = lp0_ref.shape[0]
     lines = lp0_ref.shape[1]
-    sub = dem_ref.shape[1]
+    sub = dem_ref.shape[2]
+    gens = disp_ref.shape[1]
+    relay = nb == 8
+    half = scen // 2
     s_count = n * cap
     partner = i + 1 - 2 * (i % 2)
 
@@ -82,10 +72,8 @@
     def _(m):
         pcopy(m).start()
 
-    dloc = pltpu.make_async_copy(dem_ref, dem.at[i], dloc_sem.at[0])
+    dloc = pltpu.make_async_copy(dem_ref.at[:, 0, :], dem.at[i], dloc_sem.at[0])
     dloc.start()
-    ploc = pltpu.make_async_copy(pack_ref.at[me], pin.at[me], dloc_sem.at[1])
-    ploc.start()
 
     barrier = pltpu.get_barrier_semaphore()
 
@@ -94,11 +82,13 @@
         d = (me + k) % n
         pl.semaphore_signal(barrier, inc=1, device_id=(d // nz, d % nz), device_id_type=MESH)
 
+    hot = pack_rows(nb, nz, sub, disp_ref, par_ref, bus_ref, pack)
+    dloc.wait()
     pl.semaphore_wait(barrier, n - 1)
 
     def acopy(d, s):
         return pltpu.make_async_remote_copy(
-            src_ref=pack_ref.at[d], dst_ref=pin.at[s], send_sem=a_send.at[d], recv_sem=a_recv.at[s],
+            src_ref=pack.at[d], dst_ref=pin.at[s], send_sem=a_send.at[d], recv_sem=a_recv.at[s],
             device_id=(d // nz, d % nz), device_id_type=MESH,
         )
 
@@ -106,30 +96,68 @@
     def _(k):
         acopy((me + k) % n, me).start()
 
-    def dcopy(m):
+    rows_of = (slice(0, half), slice(half, scen))
+
+    def dcopy(m, h):
         to = flip(i, m, bits)
         return pltpu.make_async_remote_copy(
-            src_ref=dem_ref, dst_ref=dem.at[i], send_sem=dem_send.at[m], recv_sem=dem_recv.at[i],
+            src_ref=dem.at[i, rows_of[h]], dst_ref=dem.at[i, rows_of[h]],
+            send_sem=dem_send.at[m, h], recv_sem=dem_recv.at[m, h],
             device_id=(to, j), device_id_type=MESH,
         )
 
-    def fcopy(m):
-        o = flip(i, m, bits)
-        return pltpu.make_async_remote_copy(
-            src_ref=dem.at[o], dst_ref=dem.at[o], send_sem=fw_send.at[m], recv_sem=dem_recv.at[o],
+    def dwait(m, h):
+        o = flip(i, m, bits)
+        return pltpu.make_async_remote_copy(
+            src_ref=dem.at[o, rows_of[h]], dst_ref=dem.at[o, rows_of[h]],
+            send_sem=dem_send.at[m, h], recv_sem=dem_recv.at[m, h],
+            device_id=(o, j), device_id_type=MESH,
+        )
+
+    def fcopy(m, h):
+        o = flip(i, m, bits)
+        return pltpu.make_async_remote_copy(
+            src_ref=dem.at[o, rows_of[h]], dst_ref=dem.at[o, rows_of[h]],
+            send_sem=fw_send.at[m, h], recv_sem=fw_recv.at[m, h],
             device_id=(partner, j), device_id_type=MESH,
         )
 
-    dcopy(1).start()
-    for m in range(2, nb, 2):
-        dcopy(m).start()
+    def fwait(m, h):
+        o = flip(i, m + 1, bits)
+        return pltpu.make_async_remote_copy(
+            src_ref=dem.at[o, rows_of[h]], dst_ref=dem.at[o, rows_of[h]],
+            send_sem=fw_send.at[m, h], recv_sem=fw_recv.at[m, h],
+            device_id=(partner, j), device_id_type=MESH,
+        )
+
+    def relay_copy(m, h):
+        o = flip(i, m, bits)
+        return pltpu.make_async_remote_copy(
+            src_ref=dem.at[o, rows_of[h]], dst_ref=dem.at[o, rows_of[h]],
+            send_sem=rel_send.at[h], recv_sem=dem_recv.at[6, h],
+            device_id=(flip(i, 6 - m, bits), j), device_id_type=MESH,
+        )
+
+    if relay:
+        dcopy(2, 0).start()
+        dcopy(4, 1).start()
+        dcopy(2, 1).start()
+        dcopy(4, 0).start()
+    else:
+        @pl.loop(1, nb // 2)
+        def _(k):
+            for h in range(2):
+                dcopy(2 * k, h).start()
+
+    for h in range(2):
+        fcopy(0, h).start()
 
     @pl.loop(1, n)
     def _(k):
         s = (me + k) % n
         acopy(s, s).wait_recv()
 
-    ploc.wait()
+    pin[me] = pack[me]
     if cap == ROWS:
         slots[...] = pin[...].reshape(s_count, LANES)
     else:
@@ -145,7 +173,7 @@
         to = flip(i, m, bits)
         return pltpu.make_async_remote_copy(
             src_ref=dbuf.at[it, i], dst_ref=dbuf.at[it, i],
-            send_sem=d_send.at[it, m], recv_sem=d_recv.at[it, i],
+            send_sem=d_send.at[it, m], recv_sem=d_recv.at[it, m],
             device_id=(to, j), device_id_type=MESH,
         )
 
@@ -153,15 +181,26 @@
         o = flip(i, m, bits)
         return pltpu.make_async_remote_copy(
             src_ref=dbuf.at[it, o], dst_ref=dbuf.at[it, o],
-            send_sem=d_send.at[it, m], recv_sem=d_recv.at[it, o],
+            send_sem=d_send.at[it, m], recv_sem=d_recv.at[it, m],
             device_id=(o, j), device_id_type=MESH,
         )
 
-    @pl.loop(1, nb)
-    def _(m):
-        gcopy(0, m).start()
-
-    dloc.wait()
+    def gforward(it, m):
+        o = flip(i, m, bits)
+        return pltpu.make_async_remote_copy(
+            src_ref=dbuf.at[it, o], dst_ref=dbuf.at[it, o],
+            send_sem=df_send.at[it, m], recv_sem=d_recv.at[it, m + 1],
+            device_id=(partner, j), device_id_type=MESH,
+        )
+
+    def gstart(it):
+        @pl.loop(1, nb // 2)
+        def _(k):
+            gcopy(it, nb - 2 * k).start()
+
+        gcopy(it, 1).start()
+
+    gstart(0)
     lf[...] = jnp.zeros_like(lf)
     lane = lax.broadcasted_iota(jnp.int32, (s_count, LANES), 1)
     at_lane = lax.broadcasted_iota(jnp.int32, (s_count, kt), 1).astype(jnp.float32) + 1.0
@@ -170,13 +209,46 @@
     def _(m):
         o = flip(i, m, bits)
 
-        @pl.when(m > 0)
+        if relay:
+            @pl.when(m == 2)
+            def _():
+                dwait(2, 0).wait_recv()
+                relay_copy(2, 0).start()
+                dwait(4, 1).wait_recv()
+                relay_copy(4, 1).start()
+                dwait(2, 1).wait_recv()
+                for h in range(2):
+                    fcopy(2, h).start()
+
+            @pl.when(m == 3)
+            def _():
+                dwait(4, 0).wait_recv()
+                for h in range(2):
+                    fcopy(4, h).start()
+
+        else:
+            @pl.when((m > 0) & (m % 2 == 0))
+            def _():
+                for h in range(2):
+                    dwait(m, h).wait_recv()
+                    fcopy(m, h).start()
+
+        @pl.when(m == nb - 2)
         def _():
-            fcopy(m).wait_recv()
-
-        @pl.when((m > 0) & (m % 2 == 0))
+            @pl.loop(1, nb // 2)
+            def _(k):
+                gwait(0, 2 * k).wait_recv()
+                gforward(0, 2 * k).start()
+
+            if relay:
+                for h in range(2):
+                    dwait(6, h).wait_recv()
+                    fcopy(6, h).start()
+
+        @pl.when(m % 2 == 1)
         def _():
-            fcopy(m).start()
+            for h in range(2):
+                fwait(m - 1, h).wait_recv()
 
         pcopy(m).wait()
         codes = jnp.sum(jnp.where(lane == LANES - nb + o, slots[...], 0.0), axis=1, keepdims=True)
@@ -215,10 +287,28 @@
 
         add_flow(0)
 
-        @pl.loop(1, nb)
-        def _(m, it=it):
-            gwait(it, m).wait_recv()
-            add_flow(m)
+        if it > 0:
+            gwait(it, 1).wait_recv()
+            add_flow(1)
+
+            @pl.loop(1, nb // 2)
+            def _(k, it=it):
+                gwait(it, 2 * k).wait_recv()
+                gforward(it, 2 * k).start()
+                add_flow(2 * k)
+
+            @pl.loop(1, nb // 2)
+            def _(k, it=it):
+                gwait(it, 2 * k + 1).wait_recv()
+                add_flow(2 * k + 1)
+        else:
+            @pl.loop(1, nb)
+            def _(m, it=it):
+                @pl.when(m % 2 == 1)
+                def _():
+                    gwait(it, m).wait_recv()
+
+                add_flow(m)
 
         def zcopy(k, it=it):
             to = (j + k) % nz
@@ -255,49 +345,52 @@
             both = dot(rhl, ghi[o], NT)
             return both[scen:, :] + dot(rh, glo[o], NT) + both[0:scen, :]
 
+        def pxcopy(m, it=it):
+            return pltpu.make_async_remote_copy(
+                src_ref=pps.at[m], dst_ref=ppx.at[it, m // 2],
+                send_sem=px_send.at[it, m // 2], recv_sem=px_recv.at[it, m // 2],
+                device_id=(partner, j), device_id_type=MESH,
+            )
+
         def ppcopy(m, it=it):
             o = flip(i, m, bits)
             return pltpu.make_async_remote_copy(
-                src_ref=pps.at[o], dst_ref=ppr.at[it, i],
-                send_sem=pp_send.at[it, m], recv_sem=pp_recv.at[it, i],
+                src_ref=pps.at[m], dst_ref=ppr.at[it, m // 2],
+                send_sem=pp_send.at[it, m // 2], recv_sem=pp_recv.at[it, m // 2],
                 device_id=(o, j), device_id_type=MESH,
             )
 
-        def ppwait(m, it=it):
-            o = flip(i, m, bits)
-            return pltpu.make_async_remote_copy(
-                src_ref=pps.at[o], dst_ref=ppr.at[it, o],
-                send_sem=pp_send.at[it, m], recv_sem=pp_recv.at[it, o],
-                device_id=(o, j), device_id_type=MESH,
-            )
-
-        @pl.loop(0, nb - 1)
+        @pl.loop(0, nb // 2)
         def _(k):
-            m = nb - 1 - k
-            o = flip(i, m, bits)
-            pps[o] = slot_price(o)
+            m = nb - 1 - 2 * k
+            pps[m] = slot_price(flip(i, m, bits))
+            pxcopy(m).start()
+
+        @pl.loop(0, nb // 2 - 1)
+        def _(k):
+            m = nb - 2 - 2 * k
+            term = slot_price(flip(i, m, bits))
+            pxcopy(m + 1).wait_recv()
+            pps[m] = term + ppx[it, m // 2]
             ppcopy(m).start()
 
-        ppr[it, i] = slot_price(i)
-
-        @pl.loop(1, nb)
-        def _(m):
-            ppwait(m).wait_recv()
-            ppcopy(m).wait_send()
-
-        unit = ppr[it, 0]
-        for s in range(1, nb):
-            unit = unit + ppr[it, s]
+        unit = slot_price(i)
+        pxcopy(1).wait_recv()
+        unit = unit + ppx[it, 0]
+        for k in range(1, nb // 2):
+            ppcopy(2 * k).wait_recv()
+            unit = unit + ppr[it, k]
+        for k in range(nb // 2):
+            pxcopy(2 * k + 1).wait_send()
+            if k:
+                ppcopy(2 * k).wait_send()
         held = dbuf[it, i]
         held = jnp.clip(
             (held - primal_step * (lin + unit)) / (1.0 + primal_step * quad), 0.0, gmax
         )
         if it < ITERS - 1:
             dbuf[it + 1, i] = held
-
-            @pl.loop(1, nb)
-            def _(m, it=it):
-                gcopy(it + 1, m).start()
+            gstart(it + 1)
 
     lp_ref[...] = price
     back = jnp.concatenate([held, jnp.zeros((LANES - scen, s_count), jnp.float32)], axis=0).T
@@ -319,15 +412,28 @@
     def _(k):
         rcopy((me + k) % n, me).start()
 
-    dcopy(1).wait_send()
-    for m in range(2, nb, 2):
-        dcopy(m).wait_send()
-        fcopy(m).wait_send()
-
-    @pl.loop(1, nb)
-    def _(m):
+    for h in range(2):
+        fcopy(0, h).wait_send()
+    if relay:
+        relay_copy(2, 0).wait_send()
+        relay_copy(4, 1).wait_send()
+    direct = 2 if relay else nb // 2 - 1
+
+    @pl.loop(1, nb // 2)
+    def _(k):
+        for h in range(2):
+            fcopy(2 * k, h).wait_send()
+
+            @pl.when(k <= direct)
+            def _(h=h):
+                dcopy(2 * k, h).wait_send()
+
         for it in range(ITERS):
-            gcopy(it, m).wait_send()
+            gcopy(it, 2 * k).wait_send()
+            gforward(it, 2 * k).wait_send()
+
+    for it in range(ITERS):
+        gcopy(it, 1).wait_send()
 
     for it in range(ITERS):
         for k in range(1, nz):
@@ -337,7 +443,7 @@
                 device_id=(i, (j + k) % nz), device_id_type=MESH,
             ).wait_send()
 
-    ret_ref[me] = rout[me]
+    rin[me] = rout[me]
 
     @pl.loop(1, n)
     def _(k):
@@ -345,7 +451,51 @@
         acopy(d, d).wait_send()
         rcopy(d, d).wait_recv()
         rcopy(d, d).wait_send()
-        ret_ref[d] = rin[d]
+
+    home = rin[...].reshape(n * ROWS, LANES).T[0:scen, :]
+    out_ref[...] = exact(home, hot, NN)
+
+
+def exact(x, hot, dims):
+    hi, lo = split(x)
+    lo2 = (x - hi.astype(jnp.float32) - lo.astype(jnp.float32)).astype(jnp.bfloat16)
+    return (dot(hi, hot, dims) + dot(lo, hot, dims)) + dot(lo2, hot, dims)
+
+
+def pack_rows(nb, nz, sub, disp_ref, par_ref, bus_ref, pack):
+    scen, gens = disp_ref.shape
+    n = nb * nz
+    f32, bf16 = jnp.float32, jnp.bfloat16
+    bus = bus_ref[...].astype(f32)
+    cell = jnp.floor((bus + 0.5) * (1.0 / sub))
+    code = bus - cell * sub + 1.0
+    block = jnp.floor((cell + 0.5) * (1.0 / nb))
+    piece = cell - block * nb
+    owner = piece * nz + block
+    owner_col = jnp.broadcast_to(owner, (LANES, gens)).T[:, 0:1]
+    same = owner_col == owner
+    earlier = lax.broadcasted_iota(jnp.int32, (gens, gens), 0) < lax.broadcasted_iota(
+        jnp.int32, (gens, gens), 1
+    )
+    rank = jnp.sum(jnp.where(same & earlier, 1.0, 0.0), axis=0, keepdims=True)
+    row = lax.broadcasted_iota(jnp.int32, (n * ROWS, gens), 0)
+    hot = jnp.where(row.astype(f32) == owner * ROWS + rank, 1.0, 0.0).astype(bf16)
+    per = nz * ROWS
+    hot_codes = jnp.where((row % per).astype(f32) == block * ROWS + rank, 1.0, 0.0).astype(bf16)
+    holder = lax.broadcasted_iota(jnp.int32, (nb, gens), 0).astype(f32)
+    codes = jnp.concatenate(
+        [jnp.zeros((LANES - nb, gens), f32), jnp.where(holder == piece, code, 0.0)], axis=0
+    )
+    body = jnp.concatenate(
+        [disp_ref[...], par_ref[...], jnp.zeros((LANES - scen - ROWS, gens), f32)], axis=0
+    )
+    hi, lo = split(body)
+    lo2 = (body - hi.astype(f32) - lo.astype(f32)).astype(bf16)
+    tile = (dot(hot, hi, NT) + dot(hot, lo, NT)) + dot(hot, lo2, NT)
+    ch, cl = split(codes)
+    tile = tile + (dot(hot_codes, ch, NT) + dot(hot_codes, cl, NT))
+    pack[...] = tile.reshape(n, ROWS, LANES)
+    return hot
 
 
 def on_device(
@@ -363,23 +513,8 @@
         cap += 1
     s_count = n * cap
     assert cap <= ROWS and scen + 4 + nb <= LANES and nb & (nb - 1) == 0
-    target, local = owner_slots(bus_map, ptdf.shape[1], sub, nz)
-    body = jnp.concatenate(
-        [
-            dispatch0,
-            cost_lin[None, :],
-            cost_quad[None, :],
-            gen_max[None, :],
-            (local + 1).astype(jnp.float32)[None, :],
-        ],
-        axis=0,
-    ).T
-    rows = jnp.zeros((n * ROWS, scen + 4), jnp.float32).at[target].set(body).reshape(n, ROWS, scen + 4)
-    codes = rows[:, :, scen + 3].reshape(nb, nz, ROWS).transpose(1, 2, 0)
-    codes = jnp.broadcast_to(codes[None], (nb, nz, ROWS, nb)).reshape(n, ROWS, nb)
-    pad = jnp.zeros((n, ROWS, LANES - nb - scen - 4), jnp.float32)
-    pack = jnp.concatenate([rows, pad, codes], axis=2)
-
+    params = jnp.stack([cost_lin, cost_quad, gen_max])
+    params = jnp.pad(params, ((0, ROWS - params.shape[0]), (0, 0)))
     depth = min(nb, 8)
     kt = sub
     while kt > 1024:
@@ -389,17 +524,19 @@
     if sub % 1024 == 0:
         kt = 1024
     f32, bf16 = jnp.float32, jnp.bfloat16
+    anywhere = pl.BlockSpec(memory_space=pl.ANY)
     vmem = pl.BlockSpec(memory_space=pltpu.VMEM)
     dma = pltpu.SemaphoreType.DMA
-    ret, line_price = pl.pallas_call(
+    return pl.pallas_call(
         functools.partial(market_kernel, nb, nz, cap, depth, kt),
         out_shape=(
-            jax.ShapeDtypeStruct((n, ROWS, LANES), f32),
+            jax.ShapeDtypeStruct((scen, gens), f32),
             jax.ShapeDtypeStruct((scen, lines), f32),
         ),
-        in_specs=[vmem, vmem, pl.BlockSpec(memory_space=pl.ANY), vmem, vmem],
+        in_specs=[vmem, vmem, vmem, anywhere, anywhere, vmem, vmem],
         out_specs=(vmem, vmem),
         scratch_shapes=[
+            pltpu.VMEM((n, ROWS, LANES), f32),
             pltpu.VMEM((n, ROWS, LANES), f32),
             pltpu.VMEM((s_count, LANES), f32),
             pltpu.VMEM((nb, scen, sub), f32),
@@ -412,24 +549,24 @@
             pltpu.VMEM((ITERS, nz, scen, lines), f32),
             pltpu.VMEM((ITERS, nb, scen, s_count), f32),
             pltpu.VMEM((nb, scen, s_count), f32),
-            pltpu.VMEM((ITERS, nb, scen, s_count), f32),
+            pltpu.VMEM((ITERS, nb // 2, scen, s_count), f32),
+            pltpu.VMEM((ITERS, nb // 2, scen, s_count), f32),
             pltpu.VMEM((n, ROWS, LANES), f32),
             pltpu.VMEM((n, ROWS, LANES), f32),
             dma((2,)), dma((depth,)),
             dma((n,)), dma((n,)),
-            dma((nb,)), dma((nb,)), dma((nb,)),
+            dma((nb, 2)), dma((nb, 2)), dma((nb, 2)), dma((nb, 2)), dma((2,)),
             dma((ITERS, nz)), dma((ITERS, nz)),
-            dma((ITERS, nb)), dma((ITERS, nb)),
-            dma((ITERS, nb)), dma((ITERS, nb)),
+            dma((ITERS, nb)), dma((ITERS, nb)), dma((ITERS, nb)),
+            dma((ITERS, nb // 2)), dma((ITERS, nb // 2)),
+            dma((ITERS, nb // 2)), dma((ITERS, nb // 2)),
             dma((n,)), dma((n,)),
         ],
         compiler_params=pltpu.CompilerParams(
             collective_id=0, has_side_effects=True, vmem_limit_bytes=60 * 1024 * 1024
         ),
         name="market",
-    )(pack, demand[:, 0, :], ptdf, line_price0, flow_max[None, :])
-    dispatch = ret.reshape(n * ROWS, LANES)[target][:, :scen].T
-    return (dispatch, line_price)
+    )(dispatch0, params, bus_map[None, :], demand, ptdf, line_price0, flow_max[None, :])
 
 
 def solution(mesh):

time: 110 us -> 97.6 us (0.89)
  Pallas kernels: 98.5 us -> 92.5 us
  local copies, waits for them, and re-layouts: 8.92 us -> 2.95 us
    pallas_call x1, Pallas kernels: 98.5 us -> 92.5 us  [on_device(): pl.pallas_call(functools.partial(market_kernel, nb, nz, cap, depth, kt),...]
    concatenate x2 -> x0, local copies, waits for them, and re-layouts: 1.65 us -> none  [the longest x1 1.58 us: on_device(): jnp.concatenate([dispatch0, cost_lin[None, :], cost_quad[None, :], gen_ma...]
    gather x1 -> x0, local copies, waits for them, and re-layouts: 1.58 us -> none  [on_device(): dispatch = ret.reshape(n * ROWS, LANES)[target][:, :scen].T]
    unnamed x3 -> x2, local copies, waits for them, and re-layouts: 4.34 us -> 2.95 us
    another operation x0 -> x1, other arithmetic: none -> 1.32 us  [on_device(): params = jnp.stack([cost_lin, cost_quad, gen_max])]
where the time goes in v2:
time: 97.6 us; the launch traced here: 97.4 us
  Pallas kernels  92.5 us (95%)
  local copies, waits for them, and re-layouts  2.95 us (3%)
  other arithmetic  1.32 us (1%)
    pallas_call x1, Pallas kernels, on_device(): pl.pallas_call(functools.partial(market_kernel, nb, nz, cap, depth, kt),...  92.5 us
    unnamed x2, local copies, waits for them, and re-layouts  2.95 us

profile of v2, /device:TPU:0, one launch (start us, length us, event | category | flops | bytes accessed | tf_op | source)
XLA Modules:
  0.0 97.4 jit_solution(14326020833456234710)
XLA Ops:
  0.6 1.3 %select_maximum_fusion.par_ref = f32[8,160]{1,0:T(8,128)} fusion(f32[1,160]{1,0:T(1,128)} %bitcast.7, f32[1,160]{1,0:T(1,128)} %bitcast.8, f32[1,160]{1,0:T(1,128)} %bitcast.9), kind=kLoop, calls=%fused_computation | loop fusion | flops 7680 | bytes 7040 | tf_op jit(solution)/shard_map/stack | solution.py:516
  1.9 92.5 %market.1 = (f32[64,160]{1,0:T(8,128)}, f32[64,256]{1,0:T(8,128)}) custom-call(f32[64,160]{1,0:T(8,128)} %disp_ref.1, f32[8,160]{1,0:T(8,128)} %select_maximum_fusion.par_ref, s32[1,160]{1,0:T(1,128)} %bitcast.5, f32[64,1,3072]{2,1,0:T(1,128)} %dem_ref.1, f32[256,24576]{1,0:T(8,128)} %ptdf_ref.1, f32[64,256]{1,0:T(8,128)} %lp0_ref.1, f32[1,256]{1,0:T(1,128)} %bitcast.6), custom_call_target="tpu_custom_call" | custom-call | tf_op jit(solution)/shard_map/market/pallas_call | solution.py:530
  94.4 1.5 %copy.13 = f32[64,160]{1,0:T(8,128)} copy(f32[64,160]{1,0:T(8,128)} %get-tuple-element.4) | data formatting | bytes 81920
  95.9 1.5 %copy.14 = f32[64,256]{1,0:T(8,128)} copy(f32[64,256]{1,0:T(8,128)} %get-tuple-element.5) | data formatting | bytes 131072

commit v3 on v2

--- a/solution.py
+++ b/solution.py
@@ -169,38 +169,48 @@
     gmax = pack_t[scen + 2:scen + 3, :]
     dbuf[0, i] = pack_t[0:scen, :]
 
-    def gcopy(it, m):
+    def gcopy(it, m, h):
         to = flip(i, m, bits)
         return pltpu.make_async_remote_copy(
-            src_ref=dbuf.at[it, i], dst_ref=dbuf.at[it, i],
-            send_sem=d_send.at[it, m], recv_sem=d_recv.at[it, m],
+            src_ref=dbuf.at[it, i, rows_of[h]], dst_ref=dbuf.at[it, i, rows_of[h]],
+            send_sem=d_send.at[2 * it + h, m], recv_sem=d_recv.at[2 * it + h, m],
             device_id=(to, j), device_id_type=MESH,
         )
 
-    def gwait(it, m):
-        o = flip(i, m, bits)
-        return pltpu.make_async_remote_copy(
-            src_ref=dbuf.at[it, o], dst_ref=dbuf.at[it, o],
-            send_sem=d_send.at[it, m], recv_sem=d_recv.at[it, m],
+    def gwait(it, m, h):
+        o = flip(i, m, bits)
+        return pltpu.make_async_remote_copy(
+            src_ref=dbuf.at[it, o, rows_of[h]], dst_ref=dbuf.at[it, o, rows_of[h]],
+            send_sem=d_send.at[2 * it + h, m], recv_sem=d_recv.at[2 * it + h, m],
             device_id=(o, j), device_id_type=MESH,
         )
 
-    def gforward(it, m):
-        o = flip(i, m, bits)
-        return pltpu.make_async_remote_copy(
-            src_ref=dbuf.at[it, o], dst_ref=dbuf.at[it, o],
-            send_sem=df_send.at[it, m], recv_sem=d_recv.at[it, m + 1],
+    def gforward(it, m, h):
+        o = flip(i, m, bits)
+        return pltpu.make_async_remote_copy(
+            src_ref=dbuf.at[it, o, rows_of[h]], dst_ref=dbuf.at[it, o, rows_of[h]],
+            send_sem=df_send.at[2 * it + h, m], recv_sem=d_recv.at[2 * it + h, m + 1],
             device_id=(partner, j), device_id_type=MESH,
         )
 
-    def gstart(it):
+    def gstart(it, h):
         @pl.loop(1, nb // 2)
         def _(k):
-            gcopy(it, nb - 2 * k).start()
-
-        gcopy(it, 1).start()
-
-    gstart(0)
+            gcopy(it, nb - 2 * k, h).start()
+
+        gcopy(it, 1, h).start()
+
+    for h in range(2):
+        gstart(0, h)
+
+    def slot_flow(it, m, r):
+        o = flip(i, m, bits)
+        dh, dl = split(dbuf[it, o, r])
+        both = dot(jnp.concatenate([dh, dl], axis=0), ghi[o], NN)
+        size = both.shape[0] // 2
+        return both[size:, :] + dot(dh, glo[o], NN) + both[0:size, :]
+
+    every = slice(0, scen)
     lf[...] = jnp.zeros_like(lf)
     lane = lax.broadcasted_iota(jnp.int32, (s_count, LANES), 1)
     at_lane = lax.broadcasted_iota(jnp.int32, (s_count, kt), 1).astype(jnp.float32) + 1.0
@@ -237,8 +247,22 @@
         def _():
             @pl.loop(1, nb // 2)
             def _(k):
-                gwait(0, 2 * k).wait_recv()
-                gforward(0, 2 * k).start()
+                for h in range(2):
+                    gwait(0, 2 * k, h).wait_recv()
+                    gforward(0, 2 * k, h).start()
+
+            for h in range(2):
+                gwait(0, 1, h).wait_recv()
+            zbuf[0, j] = slot_flow(0, 0, every)
+
+            @pl.loop(1, nb - 2)
+            def _(q):
+                @pl.when((q > 1) & (q % 2 == 1))
+                def _():
+                    for h in range(2):
+                        gwait(0, q, h).wait_recv()
+
+                zbuf[0, j] += slot_flow(0, q, every)
 
             if relay:
                 for h in range(2):
@@ -273,127 +297,136 @@
         def _():
             pcopy(m + depth).start()
 
-    price = lp0_ref[...]
     bound = dual_step * fmax_ref[...]
+    price = [lp0_ref[r, :] for r in rows_of]
+    held = [None, None]
+
+    def zcopy(it, k, h):
+        to = (j + k) % nz
+        return pltpu.make_async_remote_copy(
+            src_ref=zbuf.at[it, j, rows_of[h]], dst_ref=zbuf.at[it, j, rows_of[h]],
+            send_sem=z_send.at[2 * it + h, k], recv_sem=z_recv.at[2 * it + h, j],
+            device_id=(i, to), device_id_type=MESH,
+        )
+
+    def zwait(it, k, h):
+        o = (j + k) % nz
+        return pltpu.make_async_remote_copy(
+            src_ref=zbuf.at[it, o, rows_of[h]], dst_ref=zbuf.at[it, o, rows_of[h]],
+            send_sem=z_send.at[2 * it + h, k], recv_sem=z_recv.at[2 * it + h, o],
+            device_id=(i, o), device_id_type=MESH,
+        )
+
+    def pxcopy(it, m, h):
+        return pltpu.make_async_remote_copy(
+            src_ref=pps.at[m, rows_of[h]], dst_ref=ppx.at[it, m // 2, rows_of[h]],
+            send_sem=px_send.at[2 * it + h, m // 2], recv_sem=px_recv.at[2 * it + h, m // 2],
+            device_id=(partner, j), device_id_type=MESH,
+        )
+
+    def ppcopy(it, m, h):
+        o = flip(i, m, bits)
+        return pltpu.make_async_remote_copy(
+            src_ref=pps.at[m, rows_of[h]], dst_ref=ppr.at[it, m // 2, rows_of[h]],
+            send_sem=pp_send.at[2 * it + h, m // 2], recv_sem=pp_recv.at[2 * it + h, m // 2],
+            device_id=(o, j), device_id_type=MESH,
+        )
+
+    def slot_price(o, ref):
+        rh, rhl = ref
+        both = dot(rhl, ghi[o], NT)
+        return both[half:, :] + dot(rh, glo[o], NT) + both[0:half, :]
 
     for it in range(ITERS):
-        zbuf[it, j] = -lf[...]
-
-        def add_flow(m, it=it):
-            o = flip(i, m, bits)
-            dh, dl = split(dbuf[it, o])
-            both = dot(jnp.concatenate([dh, dl], axis=0), ghi[o], NN)
-            zbuf[it, j] += both[scen:, :] + dot(dh, glo[o], NN) + both[0:scen, :]
-
-        add_flow(0)
-
-        if it > 0:
-            gwait(it, 1).wait_recv()
-            add_flow(1)
-
-            @pl.loop(1, nb // 2)
-            def _(k, it=it):
-                gwait(it, 2 * k).wait_recv()
-                gforward(it, 2 * k).start()
-                add_flow(2 * k)
-
-            @pl.loop(1, nb // 2)
-            def _(k, it=it):
-                gwait(it, 2 * k + 1).wait_recv()
-                add_flow(2 * k + 1)
+        if it == 0:
+            for m in range(nb - 2, nb):
+                for h in range(2):
+                    if m % 2:
+                        gwait(0, m, h).wait_recv()
+                zbuf[0, j] += slot_flow(0, m, every)
+            zbuf[0, j] -= lf[...]
+            for h in range(2):
+                for k in range(1, nz):
+                    zcopy(0, k, h).start()
         else:
-            @pl.loop(1, nb)
-            def _(m, it=it):
-                @pl.when(m % 2 == 1)
-                def _():
-                    gwait(it, m).wait_recv()
-
-                add_flow(m)
-
-        def zcopy(k, it=it):
-            to = (j + k) % nz
-            return pltpu.make_async_remote_copy(
-                src_ref=zbuf.at[it, j], dst_ref=zbuf.at[it, j],
-                send_sem=z_send.at[it, k], recv_sem=z_recv.at[it, j],
-                device_id=(i, to), device_id_type=MESH,
+            for h in range(2):
+                r = rows_of[h]
+                zbuf[it, j, r] = slot_flow(it, 0, r) - lf[r, :]
+                gwait(it, 1, h).wait_recv()
+                zbuf[it, j, r] += slot_flow(it, 1, r)
+
+                @pl.loop(1, nb // 2)
+                def _(k, it=it, h=h, r=r):
+                    gwait(it, 2 * k, h).wait_recv()
+                    gforward(it, 2 * k, h).start()
+                    zbuf[it, j, r] += slot_flow(it, 2 * k, r)
+
+            for h in range(2):
+                r = rows_of[h]
+
+                @pl.loop(1, nb // 2)
+                def _(k, it=it, h=h, r=r):
+                    gwait(it, 2 * k + 1, h).wait_recv()
+                    zbuf[it, j, r] += slot_flow(it, 2 * k + 1, r)
+
+                for k in range(1, nz):
+                    zcopy(it, k, h).start()
+
+        moved = []
+        for h in range(2):
+            r = rows_of[h]
+            for k in range(1, nz):
+                zwait(it, k, h).wait_recv()
+            flow = zbuf[it, 0, r]
+            for k in range(1, nz):
+                flow = flow + zbuf[it, k, r]
+            trial = price[h] + dual_step * flow
+            price_next = trial - jnp.clip(trial, -bound, bound)
+            rh, rl = split(2.0 * price_next - price[h])
+            price[h] = price_next
+            moved.append((rh, jnp.concatenate([rh, rl], axis=0)))
+
+            @pl.loop(0, nb // 2)
+            def _(k, it=it, h=h, r=r, ref=moved[h]):
+                m = nb - 1 - 2 * k
+                pps[m, r] = slot_price(flip(i, m, bits), ref)
+                pxcopy(it, m, h).start()
+
+        for h in range(2):
+            r = rows_of[h]
+
+            @pl.loop(0, nb // 2 - 1)
+            def _(k, it=it, h=h, r=r, ref=moved[h]):
+                m = nb - 2 - 2 * k
+                term = slot_price(flip(i, m, bits), ref)
+                pxcopy(it, m + 1, h).wait_recv()
+                pps[m, r] = term + ppx[it, m // 2, r]
+                ppcopy(it, m, h).start()
+
+        for h in range(2):
+            r = rows_of[h]
+            unit = slot_price(i, moved[h])
+            pxcopy(it, 1, h).wait_recv()
+            unit = unit + ppx[it, 0, r]
+            for k in range(1, nb // 2):
+                ppcopy(it, 2 * k, h).wait_recv()
+                unit = unit + ppr[it, k, r]
+            held[h] = jnp.clip(
+                (dbuf[it, i, r] - primal_step * (lin + unit)) / (1.0 + primal_step * quad), 0.0, gmax
             )
-
-        def zwait(k, it=it):
-            o = (j + k) % nz
-            return pltpu.make_async_remote_copy(
-                src_ref=zbuf.at[it, o], dst_ref=zbuf.at[it, o],
-                send_sem=z_send.at[it, k], recv_sem=z_recv.at[it, o],
-                device_id=(i, o), device_id_type=MESH,
-            )
-
-        for k in range(1, nz):
-            zcopy(k).start()
-        for k in range(1, nz):
-            zwait(k).wait_recv()
-        flow = zbuf[it, 0]
-        for k in range(1, nz):
-            flow = flow + zbuf[it, k]
-        trial = price + dual_step * flow
-        price_next = trial - jnp.clip(trial, -bound, bound)
-        reflected = 2.0 * price_next - price
-        price = price_next
-
-        rh, rl = split(reflected)
-        rhl = jnp.concatenate([rh, rl], axis=0)
-
-        def slot_price(o):
-            both = dot(rhl, ghi[o], NT)
-            return both[scen:, :] + dot(rh, glo[o], NT) + both[0:scen, :]
-
-        def pxcopy(m, it=it):
-            return pltpu.make_async_remote_copy(
-                src_ref=pps.at[m], dst_ref=ppx.at[it, m // 2],
-                send_sem=px_send.at[it, m // 2], recv_sem=px_recv.at[it, m // 2],
-                device_id=(partner, j), device_id_type=MESH,
-            )
-
-        def ppcopy(m, it=it):
-            o = flip(i, m, bits)
-            return pltpu.make_async_remote_copy(
-                src_ref=pps.at[m], dst_ref=ppr.at[it, m // 2],
-                send_sem=pp_send.at[it, m // 2], recv_sem=pp_recv.at[it, m // 2],
-                device_id=(o, j), device_id_type=MESH,
-            )
-
-        @pl.loop(0, nb // 2)
-        def _(k):
-            m = nb - 1 - 2 * k
-            pps[m] = slot_price(flip(i, m, bits))
-            pxcopy(m).start()
-
-        @pl.loop(0, nb // 2 - 1)
-        def _(k):
-            m = nb - 2 - 2 * k
-            term = slot_price(flip(i, m, bits))
-            pxcopy(m + 1).wait_recv()
-            pps[m] = term + ppx[it, m // 2]
-            ppcopy(m).start()
-
-        unit = slot_price(i)
-        pxcopy(1).wait_recv()
-        unit = unit + ppx[it, 0]
-        for k in range(1, nb // 2):
-            ppcopy(2 * k).wait_recv()
-            unit = unit + ppr[it, k]
-        for k in range(nb // 2):
-            pxcopy(2 * k + 1).wait_send()
-            if k:
-                ppcopy(2 * k).wait_send()
-        held = dbuf[it, i]
-        held = jnp.clip(
-            (held - primal_step * (lin + unit)) / (1.0 + primal_step * quad), 0.0, gmax
-        )
-        if it < ITERS - 1:
-            dbuf[it + 1, i] = held
-            gstart(it + 1)
-
-    lp_ref[...] = price
-    back = jnp.concatenate([held, jnp.zeros((LANES - scen, s_count), jnp.float32)], axis=0).T
+            if it < ITERS - 1:
+                dbuf[it + 1, i, r] = held[h]
+                gstart(it + 1, h)
+
+        for h in range(2):
+            for k in range(nb // 2):
+                pxcopy(it, 2 * k + 1, h).wait_send()
+                if k:
+                    ppcopy(it, 2 * k, h).wait_send()
+
+    for h in range(2):
+        lp_ref[rows_of[h], :] = price[h]
+    back = jnp.concatenate([held[0], held[1], jnp.zeros((LANES - scen, s_count), jnp.float32)], axis=0).T
     if cap == ROWS:
         rout[...] = back.reshape(n, ROWS, LANES)
     else:
@@ -429,19 +462,15 @@
                 dcopy(2 * k, h).wait_send()
 
         for it in range(ITERS):
-            gcopy(it, 2 * k).wait_send()
-            gforward(it, 2 * k).wait_send()
+            for h in range(2):
+                gcopy(it, 2 * k, h).wait_send()
+                gforward(it, 2 * k, h).wait_send()
 
     for it in range(ITERS):
-        gcopy(it, 1).wait_send()
-
-    for it in range(ITERS):
-        for k in range(1, nz):
-            pltpu.make_async_remote_copy(
-                src_ref=zbuf.at[it, j], dst_ref=zbuf.at[it, j],
-                send_sem=z_send.at[it, k], recv_sem=z_recv.at[it, j],
-                device_id=(i, (j + k) % nz), device_id_type=MESH,
-            ).wait_send()
+        for h in range(2):
+            gcopy(it, 1, h).wait_send()
+            for k in range(1, nz):
+                zcopy(it, k, h).wait_send()
 
     rin[me] = rout[me]
 
@@ -556,10 +585,10 @@
             dma((2,)), dma((depth,)),
             dma((n,)), dma((n,)),
             dma((nb, 2)), dma((nb, 2)), dma((nb, 2)), dma((nb, 2)), dma((2,)),
-            dma((ITERS, nz)), dma((ITERS, nz)),
-            dma((ITERS, nb)), dma((ITERS, nb)), dma((ITERS, nb)),
-            dma((ITERS, nb // 2)), dma((ITERS, nb // 2)),
-            dma((ITERS, nb // 2)), dma((ITERS, nb // 2)),
+            dma((2 * ITERS, nz)), dma((2 * ITERS, nz)),
+            dma((2 * ITERS, nb)), dma((2 * ITERS, nb)), dma((2 * ITERS, nb)),
+            dma((2 * ITERS, nb // 2)), dma((2 * ITERS, nb // 2)),
+            dma((2 * ITERS, nb // 2)), dma((2 * ITERS, nb // 2)),
             dma((n,)), dma((n,)),
         ],
         compiler_params=pltpu.CompilerParams(

time: 97.6 us -> 94.2 us (0.965)
  Pallas kernels: 92.5 us -> 89.1 us
    pallas_call x1, Pallas kernels: 92.5 us -> 89.1 us  [on_device(): pl.pallas_call(functools.partial(market_kernel, nb, nz, cap, depth, kt),...]
where the time goes in v3:
time: 94.2 us; the launch traced here: 94 us
  Pallas kernels  89.1 us (95%)
  local copies, waits for them, and re-layouts  2.95 us (3%)
  other arithmetic  1.32 us (1%)
    pallas_call x1, Pallas kernels, on_device(): pl.pallas_call(functools.partial(market_kernel, nb, nz, cap, depth, kt),...  89.1 us
    unnamed x2, local copies, waits for them, and re-layouts  2.95 us

profile of v3, /device:TPU:0, one launch (start us, length us, event | category | flops | bytes accessed | tf_op | source)
XLA Modules:
  0.0 94.0 jit_solution(12550865803601682680)
XLA Ops:
  0.6 1.3 %select_maximum_fusion.par_ref = f32[8,160]{1,0:T(8,128)} fusion(f32[1,160]{1,0:T(1,128)} %bitcast.7, f32[1,160]{1,0:T(1,128)} %bitcast.8, f32[1,160]{1,0:T(1,128)} %bitcast.9), kind=kLoop, calls=%fused_computation | loop fusion | flops 7680 | bytes 7040 | tf_op jit(solution)/shard_map/stack | solution.py:545
  1.9 89.1 %market.1 = (f32[64,160]{1,0:T(8,128)}, f32[64,256]{1,0:T(8,128)}) custom-call(f32[64,160]{1,0:T(8,128)} %disp_ref.1, f32[8,160]{1,0:T(8,128)} %select_maximum_fusion.par_ref, s32[1,160]{1,0:T(1,128)} %bitcast.5, f32[64,1,3072]{2,1,0:T(1,128)} %dem_ref.1, f32[256,24576]{1,0:T(8,128)} %ptdf_ref.1, f32[64,256]{1,0:T(8,128)} %lp0_ref.1, f32[1,256]{1,0:T(1,128)} %bitcast.6), custom_call_target="tpu_custom_call" | custom-call | tf_op jit(solution)/shard_map/market/pallas_call | solution.py:559
  91.0 1.5 %copy.13 = f32[64,160]{1,0:T(8,128)} copy(f32[64,160]{1,0:T(8,128)} %get-tuple-element.4) | data formatting | bytes 81920
  92.5 1.5 %copy.14 = f32[64,256]{1,0:T(8,128)} copy(f32[64,256]{1,0:T(8,128)} %get-tuple-element.5) | data formatting | bytes 131072

commit v4 on v3

--- a/solution.py
+++ b/solution.py
@@ -40,7 +40,7 @@
 
 def market_kernel(
     nb, nz, cap, depth, kt,
-    disp_ref, par_ref, bus_ref, dem_ref, ptdf_ref, lp0_ref, fmax_ref,
+    disp_ref, lin_ref, quad_ref, gmax_ref, bus_ref, dem_ref, ptdf_ref, lp0_ref, fmax_ref,
     out_ref, lp_ref,
     pack, pin, slots, dem, pbuf, acc1, acc2, ghi, glo, lf, zbuf, dbuf, pps, ppx, ppr, rout, rin,
     dloc_sem, p_sem, a_send, a_recv, dem_send, dem_recv, fw_send, fw_recv, rel_send,
@@ -82,7 +82,7 @@
         d = (me + k) % n
         pl.semaphore_signal(barrier, inc=1, device_id=(d // nz, d % nz), device_id_type=MESH)
 
-    hot = pack_rows(nb, nz, sub, disp_ref, par_ref, bus_ref, pack)
+    hot = pack_rows(nb, nz, sub, disp_ref, (lin_ref, quad_ref, gmax_ref), bus_ref, pack)
     dloc.wait()
     pl.semaphore_wait(barrier, n - 1)
 
@@ -491,7 +491,7 @@
     return (dot(hi, hot, dims) + dot(lo, hot, dims)) + dot(lo2, hot, dims)
 
 
-def pack_rows(nb, nz, sub, disp_ref, par_ref, bus_ref, pack):
+def pack_rows(nb, nz, sub, disp_ref, par_refs, bus_ref, pack):
     scen, gens = disp_ref.shape
     n = nb * nz
     f32, bf16 = jnp.float32, jnp.bfloat16
@@ -515,8 +515,12 @@
     codes = jnp.concatenate(
         [jnp.zeros((LANES - nb, gens), f32), jnp.where(holder == piece, code, 0.0)], axis=0
     )
+    at_row = lax.broadcasted_iota(jnp.int32, (ROWS, gens), 0)
+    par = jnp.zeros((ROWS, gens), f32)
+    for k, ref in enumerate(par_refs):
+        par = jnp.where(at_row == k, ref[...], par)
     body = jnp.concatenate(
-        [disp_ref[...], par_ref[...], jnp.zeros((LANES - scen - ROWS, gens), f32)], axis=0
+        [disp_ref[...], par, jnp.zeros((LANES - scen - ROWS, gens), f32)], axis=0
     )
     hi, lo = split(body)
     lo2 = (body - hi.astype(f32) - lo.astype(f32)).astype(bf16)
@@ -542,8 +546,6 @@
         cap += 1
     s_count = n * cap
     assert cap <= ROWS and scen + 4 + nb <= LANES and nb & (nb - 1) == 0
-    params = jnp.stack([cost_lin, cost_quad, gen_max])
-    params = jnp.pad(params, ((0, ROWS - params.shape[0]), (0, 0)))
     depth = min(nb, 8)
     kt = sub
     while kt > 1024:
@@ -562,7 +564,7 @@
             jax.ShapeDtypeStruct((scen, gens), f32),
             jax.ShapeDtypeStruct((scen, lines), f32),
         ),
-        in_specs=[vmem, vmem, vmem, anywhere, anywhere, vmem, vmem],
+        in_specs=[vmem, vmem, vmem, vmem, vmem, anywhere, anywhere, vmem, vmem],
         out_specs=(vmem, vmem),
         scratch_shapes=[
             pltpu.VMEM((n, ROWS, LANES), f32),
@@ -595,7 +597,9 @@
             collective_id=0, has_side_effects=True, vmem_limit_bytes=60 * 1024 * 1024
         ),
         name="market",
-    )(dispatch0, params, bus_map[None, :], demand, ptdf, line_price0, flow_max[None, :])
+    )(
+        dispatch0, cost_lin[None, :], cost_quad[None, :], gen_max[None, :], bus_map[None, :],
+        demand, ptdf, line_price0, flow_max[None, :])
 
 
 def solution(mesh):

time: 94.2 us -> 92.9 us (0.986)
  other arithmetic: 1.32 us -> 0 us
    another operation x1 -> x0, other arithmetic: 1.32 us -> none  [on_device(): params = jnp.stack([cost_lin, cost_quad, gen_max])]
where the time goes in v4:
time: 92.9 us; the launch traced here: 92.7 us
  Pallas kernels  89.1 us (96%)
  local copies, waits for them, and re-layouts  2.95 us (3%)
    pallas_call x1, Pallas kernels, on_device(): pl.pallas_call(functools.partial(market_kernel, nb, nz, cap, depth, kt),...  89.1 us
    unnamed x2, local copies, waits for them, and re-layouts  2.95 us

profile of v4, /device:TPU:0, one launch (start us, length us, event | category | flops | bytes accessed | tf_op | source)
XLA Modules:
  0.0 92.7 jit_solution(18081804787394502051)
XLA Ops:
  0.6 89.1 %market.1 = (f32[64,160]{1,0:T(8,128)}, f32[64,256]{1,0:T(8,128)}) custom-call(f32[64,160]{1,0:T(8,128)} %disp_ref.1, f32[1,160]{1,0:T(1,128)} %bitcast.5, f32[1,160]{1,0:T(1,128)} %bitcast.6, f32[1,160]{1,0:T(1,128)} %bitcast.7, s32[1,160]{1,0:T(1,128)} %bitcast.8, f32[64,1,3072]{2,1,0:T(1,128)} %dem_ref.1, f32[256,24576]{1,0:T(8,128)} %ptdf_ref.1, ...), custom_call_target="tpu_custom_call" | custom-call | tf_op jit(solution)/shard_map/market/pallas_call | solution.py:561
  89.7 1.5 %copy.13 = f32[64,160]{1,0:T(8,128)} copy(f32[64,160]{1,0:T(8,128)} %get-tuple-element.4) | data formatting | bytes 81920
  91.2 1.5 %copy.14 = f32[64,256]{1,0:T(8,128)} copy(f32[64,256]{1,0:T(8,128)} %get-tuple-element.5) | data formatting | bytes 131072
